TPU v7x, 32 devices: a whole 2x2x4 slice. The times are simulated.
32 devices in a mesh: op: 4 (over y, x), str: 8 (over z, core).
Axes of the slice: x: 2, y: 2, z: 4, core: 2. Of those that a mesh axis runs over, the one named last changes fastest.
Arguments:
- coeffs: float32 [4096, 4096], P('str'), may hold values from -6 to 6
- previous: float32 [4096, 4096], P('str'), may hold values from -6 to 6
- block_values: bfloat16 [4, 32, 6, 128, 128], P('op'), may hold values from -0.21875 to 0.21875
- block_cols: int32 [4, 32, 6], P('op'), may hold values from 0 to 31, as said below
Outputs:
- advanced: float32 [4096, 4096], P('str')
Inputs may be any that keep to these rules, and one draw needn't show every extreme that they name: For every term k and block row r, block_cols[k, r, 0] equals r and the 6 entries of block_cols[k, r] are distinct.
All inputs are finite; a program needn't handle non-finite values.
Results may differ from a plain program's by a relative error of at most 0.0003.
Values sent between devices are 32-bit elements; how exact they have to be, the bound alone decides.
A program may use at most 192 MiB of HBM per device.

v0:
```python
import math
import jax
import jax.numpy as jnp
from jax import lax
from jax.sharding import PartitionSpec as P

STEPS = 2


def per_device(coeffs, previous, block_values, block_cols):
    local_terms = block_values.shape[0]
    step_scale = 2.0 / math.sqrt(local_terms * lax.axis_size("op"))
    factors = block_values.astype(jnp.float32)
    row_count, full_width = coeffs.shape
    block_size = block_values.shape[-1]
    block_count = full_width // block_size
    slot_count = block_cols.shape[2]
    regrouped = lax.all_to_all(
        previous.reshape(row_count, block_count, block_size),
        "str",
        split_axis=1,
        concat_axis=0,
        tiled=True,
    )
    earlier = regrouped.reshape(full_width, row_count).T
    current = coeffs
    for step_index in range(STEPS):
        column_list = block_cols[0].reshape(-1)
        term_factors = factors[0]
        gathered = jnp.take(
            current.reshape(row_count, block_count, block_size), column_list, axis=1
        )
        gathered = gathered.reshape(row_count, block_count, slot_count, block_size)
        beta_side = jnp.einsum(
            "arjc,rjoc->aro", gathered, term_factors, precision=lax.Precision.HIGHEST
        )
        received = lax.all_to_all(beta_side, "str", split_axis=1, concat_axis=0, tiled=True)
        group_count = received.shape[1]
        item_count = received.shape[2]
        grouped = jnp.take(
            received.reshape(block_count, block_size, group_count, item_count), column_list, axis=0
        )
        grouped = grouped.reshape(block_count, slot_count, block_size, group_count, item_count)
        result = jnp.einsum(
            "rjoc,rjcnm->nmro", term_factors, grouped, precision=lax.Precision.HIGHEST
        )
        moved = result.reshape(group_count, item_count, full_width)
        summed = moved.reshape(row_count, full_width)
        updated = step_scale * lax.psum(summed, "op") - earlier
        earlier, current = (current, updated)
    return current


def solution(mesh):
    placed = (P("str", None), P("str", None), P("op", None, None, None, None), P("op", None, None))
    return jax.shard_map(
        per_device, mesh=mesh, in_specs=placed, out_specs=P("str", None), check_vma=False
    )
```

profile of v0, /device:TPU:0, one launch (start us, length us, event | category | flops | bytes accessed | tf_op | source)
XLA Modules:
  0.0 1236.2 jit_solution(6269851794979325475)
XLA Ops:
  7.4 9.0 copy.26
  16.4 9.0 copy.27
  25.3 22.2 %gather_fusion = f32[192,512,128]{2,1,0:T(8,128)} fusion(f32[512,32,128]{2,0,1:T(8,128)} %copy.27, s32[1024]{0:T(1024)S(1)} %pad_clamp_fusion), kind=kCustom, calls=%fused_computation.clone | custom fusion | bytes 100664064 | tf_op jit(solution)/shard_map/jit(_take)/gather | solution.py:30
  47.6 34.0 %broadcast_select_fusion.3 = f32[192,512,128]{2,1,0:T(8,128)} fusion(f32[192,512,128]{2,1,0:T(8,128)} %gather_fusion, pred[192]{0:T(512)(128)(4,1)S(1)} %compare_and_fusion), kind=kLoop, calls=%fused_computation.7 | loop fusion | flops 12582912 | bytes 100663488 | tf_op jit(solution)/shard_map/jit(_take)/select_n | solution.py:30
  81.6 30.1 %fusion.8 = f32[512,32,128]{2,0,1:T(8,128)} fusion(f32[512,32,6,128]{3,0,2,1:T(8,128)} %bitcast.92, bf16[1,32,6,128,128]{4,3,2,1,0:T(8,128)(2,1)} %param.10), kind=kOutput, calls=%fused_computation.19 | convolution fusion | flops 19327352832 | bytes 65011712 | tf_op jit(solution)/shard_map/arjc,rjoc->aro/dot_general | solution.py:34
  111.7 6.4 all-to-all-start
  118.1 9.0 copy.31
  127.1 175.0 %all-to-all-done = f32[512,32,128]{2,0,1:T(8,128)} async-done(((f32[512,32,128]{2,0,1:T(8,128)}), f32[512,32,128]{2,0,1:T(8,128)}, u32[]{:S(2)}, u32[]{:S(2)}) %all-to-all-start) | async-done | bytes 8388640 | tf_op jit(solution)/shard_map/all_to_all | solution.py:37
  307.1 7.7 copy.28
  314.7 22.2 %gather_fusion.1 = f32[192,128,4,128]{3,1,2,0:T(8,128)} fusion(f32[32,128,4,128]{3,1,0,2:T(8,128)} %bitcast.91, s32[1024]{0:T(1024)S(1)} %pad_clamp_fusion), kind=kCustom, calls=%fused_computation.1.clone | custom fusion | bytes 100664064 | tf_op jit(solution)/shard_map/jit(_take)/gather | solution.py:40
  337.0 34.9 %broadcast_select_fusion.1 = f32[192,128,4,128]{3,1,2,0:T(8,128)} fusion(f32[192,128,4,128]{3,1,2,0:T(8,128)} %gather_fusion.1, pred[192]{0:T(512)(128)(4,1)S(1)} %compare_and_fusion), kind=kLoop, calls=%fused_computation.5 | loop fusion | flops 12582912 | bytes 100663488 | tf_op jit(solution)/shard_map/jit(_take)/select_n | solution.py:40
  371.9 48.2 %fusion.14 = f32[4,128,32,128]{3,1,0,2:T(8,128)} fusion(f32[32,6,128,4,128]{4,2,3,1,0:T(8,128)} %bitcast.95, bf16[1,32,6,128,128]{4,3,2,1,0:T(8,128)(2,1)} %param.10), kind=kOutput, calls=%fused_computation.21 | convolution fusion | flops 19327352832 | bytes 65011712 | tf_op jit(solution)/shard_map/rjoc,rjcnm->nmro/dot_general | solution.py:44
  420.1 8.2 copy.30
  428.4 11.7 copy.55
  440.1 50.7 %all-to-all-done.1 = f32[512,32,128]{0,2,1:T(8,128)} async-done(((f32[512,32,128]{0,2,1:T(8,128)}), f32[512,32,128]{0,2,1:T(8,128)}, u32[]{:S(2)}, u32[]{:S(2)}) %all-to-all-start.1) | async-done | bytes 8388640 | tf_op jit(solution)/shard_map/all_to_all | solution.py:18
  490.9 8.4 copy.33
  499.2 11.7 copy.50
  511.0 102.6 %all-reduce.3.cloned.1.call-done = f32[512,4096]{1,0:T(8,128)} async-done(((f32[512,4096]{1,0:T(8,128)}), f32[512,4096]{1,0:T(8,128)}) %all-reduce.3.cloned.1.call-update) | async-done | bytes 8388624 | tf_op jit(solution)/shard_map/psum | solution.py:49
  613.6 11.3 bitcast_subtract_fusion
  624.9 9.0 copy.34
  633.9 8.9 copy.35
  642.8 22.2 %gather_fusion.2 = f32[192,512,128]{2,1,0:T(8,128)} fusion(f32[512,32,128]{2,0,1:T(8,128)} %copy.35, s32[1024]{0:T(1024)S(1)} %pad_clamp_fusion), kind=kCustom, calls=%fused_computation.2.clone | custom fusion | bytes 100664064 | tf_op jit(solution)/shard_map/jit(_take)/gather | solution.py:30
  665.0 34.0 %broadcast_select_fusion.2 = f32[192,512,128]{2,1,0:T(8,128)} fusion(f32[192,512,128]{2,1,0:T(8,128)} %gather_fusion.2, pred[192]{0:T(512)(128)(4,1)S(1)} %compare_and_fusion), kind=kLoop, calls=%fused_computation.6 | loop fusion | flops 12582912 | bytes 100663488 | tf_op jit(solution)/shard_map/jit(_take)/select_n | solution.py:30
  699.1 30.1 %fusion.11 = f32[512,32,128]{2,0,1:T(8,128)} fusion(f32[512,32,6,128]{3,0,2,1:T(8,128)} %bitcast.93, bf16[1,32,6,128,128]{4,3,2,1,0:T(8,128)(2,1)} %param.10), kind=kOutput, calls=%fused_computation.20 | convolution fusion | flops 19327352832 | bytes 65011712 | tf_op jit(solution)/shard_map/arjc,rjoc->aro/dot_general | solution.py:34
  729.2 188.9 %all_to_all.45 = f32[512,32,128]{2,0,1:T(8,128)S(1)} all-to-all(f32[512,32,128]{2,0,1:T(8,128)} %fusion.11), channel_id=1, replica_groups=mesh['op'=4,'str'=8] {'str'}, dimensions={1} | all-to-all | bytes 16777216 | tf_op jit(solution)/shard_map/all_to_all | solution.py:37
  922.1 22.2 %gather_fusion.3 = f32[192,128,4,128]{3,1,2,0:T(8,128)} fusion(f32[32,128,4,128]{3,1,0,2:T(8,128)} %bitcast.90, s32[1024]{0:T(1024)S(1)} %pad_clamp_fusion), kind=kCustom, calls=%fused_computation.3.clone | custom fusion | bytes 100664064 | tf_op jit(solution)/shard_map/jit(_take)/gather | solution.py:40
  944.3 34.9 %broadcast_select_fusion = f32[192,128,4,128]{3,1,2,0:T(8,128)} fusion(f32[192,128,4,128]{3,1,2,0:T(8,128)} %gather_fusion.3, pred[192]{0:T(512)(128)(4,1)S(1)} %compare_and_fusion), kind=kLoop, calls=%fused_computation.4 | loop fusion | flops 12582912 | bytes 100663488 | tf_op jit(solution)/shard_map/jit(_take)/select_n | solution.py:40
  979.3 47.8 %fusion.17 = f32[4,128,32,128]{3,1,0,2:T(8,128)} fusion(f32[32,6,128,4,128]{4,2,3,1,0:T(8,128)} %bitcast.94, bf16[1,32,6,128,128]{4,3,2,1,0:T(8,128)(2,1)} %param.10), kind=kOutput, calls=%fused_computation.22 | convolution fusion | flops 19327352832 | bytes 65011712 | tf_op jit(solution)/shard_map/rjoc,rjcnm->nmro/dot_general | solution.py:44
  1027.1 8.2 copy.38
  1035.4 11.8 copy.54
  1047.1 170.5 %all-reduce.5.cloned.1.call-done = f32[512,4096]{1,0:T(8,128)} async-done(((f32[512,4096]{1,0:T(8,128)}), f32[512,4096]{1,0:T(8,128)}) %all-reduce.5.cloned.1.call-update) | async-done | bytes 8388624 | tf_op jit(solution)/shard_map/psum | solution.py:49
  1217.6 11.3 sub.7
  (11 shorter events, 9.9 us)
Async XLA Ops:
  111.7 190.3 %all-to-all-start = ((f32[512,32,128]{2,0,1:T(8,128)}), f32[512,32,128]{2,0,1:T(8,128)}, u32[]{:S(2)}, u32[]{:S(2)}) async-start(f32[512,32,128]{2,0,1:T(8,128)} %fusion.8), calls=%async_computation | async-start | bytes 16777216 | tf_op jit(solution)/shard_map/all_to_all | solution.py:37
  302.1 188.8 %all-to-all-start.1 = ((f32[512,32,128]{0,2,1:T(8,128)}), f32[512,32,128]{0,2,1:T(8,128)}, u32[]{:S(2)}, u32[]{:S(2)}) async-start(f32[512,32,128]{0,2,1:T(8,128)} %bitcast.97), calls=%async_computation.1 | async-start | bytes 16777216 | tf_op jit(solution)/shard_map/all_to_all | solution.py:18
  307.0 306.5 %all-reduce.3.cloned.1.call-start = ((), (), s32[]{:S(2)}) async-start(), calls=%async_computation.3 | async-start | bytes 16777216 | tf_op jit(solution)/shard_map/psum | solution.py:49
  440.1 777.5 %all-reduce.5.cloned.1.call-start = ((), (), s32[]{:S(2)}) async-start(), calls=%async_computation.4 | async-start | bytes 16777216 | tf_op jit(solution)/shard_map/psum | solution.py:49
Sparse Core Ops, SparseCore 0:
  440.2 173.3 all-reduce.2
  1047.3 170.2 all-reduce.4
where the time goes:
time: 1250 us; the launch traced here: 1240 us
  waiting for transfers between devices  499 us (40%)
  local copies, waits for them, and re-layouts  206 us (16%)
  blocking collectives  189 us (15%)
  other arithmetic  161 us (13%)
  matrix products  156 us (12%)
  between operations  13.9 us (1%)
    psum x2, waiting for transfers between devices, per_device(): updated = step_scale * lax.psum(summed, 'op') - earlier  273 us
    all_to_all x1, blocking collectives, per_device(): lax.all_to_all(beta_side, 'str', split_axis=1, concat_axis=0, tiled=True)  189 us
    all_to_all x1, waiting for transfers between devices, per_device(): lax.all_to_all(beta_side, 'str', split_axis=1, concat_axis=0, tiled=True)  175 us
    dot_general x2, matrix products, per_device(): jnp.einsum('rjoc,rjcnm->nmro', term_factors, grouped, precision=lax.Preci...  96.1 us
    select_n x3, other arithmetic, per_device(): jnp.take(received.reshape(block_count, block_size, group_count, item_coun...  69.9 us
    select_n x2, other arithmetic, per_device(): jnp.take(current.reshape(row_count, block_count, block_size), column_list...  68.1 us
    dot_general x2, matrix products, per_device(): jnp.einsum('arjc,rjoc->aro', gathered, term_factors, precision=lax.Precis...  60.2 us
    unnamed x6, local copies, waits for them, and re-layouts  53.9 us
  transfers between devices with their start and end apart: 4, of which 4 were waited for; matrix products, arithmetic and copies ran while one was open for 13% of the time, Pallas kernels for 0%

commit v1 on v0

--- a/solution.py
+++ b/solution.py
@@ -5,6 +5,22 @@
 from jax.sharding import PartitionSpec as P
 
 STEPS = 2
+
+
+def pairwise_exchange(value, axis, split, join):
+    ways, here = (lax.axis_size(axis), lax.axis_index(axis))
+    width = value.shape[split] // ways
+    shape = list(value.shape)
+    shape[split] = width
+    height = shape[join]
+    shape[join] = height * ways
+    full = jnp.zeros(shape, value.dtype)
+    for mask in range(ways):
+        part = lax.dynamic_slice_in_dim(value, (here ^ mask) * width, width, axis=split)
+        if mask:
+            part = lax.ppermute(part, axis, [(d, d ^ mask) for d in range(ways)])
+        full = lax.dynamic_update_slice_in_dim(full, part, (here ^ mask) * height, axis=join)
+    return full
 
 
 def per_device(coeffs, previous, block_values, block_cols):
@@ -34,7 +50,7 @@
         beta_side = jnp.einsum(
             "arjc,rjoc->aro", gathered, term_factors, precision=lax.Precision.HIGHEST
         )
-        received = lax.all_to_all(beta_side, "str", split_axis=1, concat_axis=0, tiled=True)
+        received = pairwise_exchange(beta_side, "str", 1, 0)
         group_count = received.shape[1]
         item_count = received.shape[2]
         grouped = jnp.take(

time: 1250 us -> 1330 us (1.064)
  waiting for transfers between devices: 499 us -> 723 us
  blocking collectives: 189 us -> 0 us
  local copies, waits for them, and re-layouts: 206 us -> 238 us
    ppermute x0 -> x14, waiting for transfers between devices: none -> 226 us  [pairwise_exchange(): part = lax.ppermute(part, axis, [(d, d ^ mask) for d in range(ways)])]
    all_to_all x1 -> x0, blocking collectives: 189 us -> none  [per_device(): lax.all_to_all(beta_side, 'str', split_axis=1, concat_axis=0, tiled=True)]
    all_to_all x1 -> x0, waiting for transfers between devices: 175 us -> none  [per_device(): lax.all_to_all(beta_side, 'str', split_axis=1, concat_axis=0, tiled=True)]
    psum x2, waiting for transfers between devices: 273 us -> 405 us  [per_device(): updated = step_scale * lax.psum(summed, 'op') - earlier]
    all_to_all x1, waiting for transfers between devices: 50.7 us -> 92.6 us  [per_device(): lax.all_to_all(previous.reshape(row_count, block_count, block_size), 'str...]
    dynamic_update_slice x0 -> x16, local copies, waits for them, and re-layouts: none -> 25.3 us  [pairwise_exchange(): lax.dynamic_update_slice_in_dim(full, part, (here ^ mask) * height, axis=...]
    ppermute x0 -> x14, starting transfers between devices: none -> 18.1 us  [pairwise_exchange(): part = lax.ppermute(part, axis, [(d, d ^ mask) for d in range(ways)])]
    unnamed x6 -> x14, local copies, waits for them, and re-layouts: 53.9 us -> 55 us
  transfers between devices with their start and end apart: 4 -> 17, of which waited for: 4 -> 8; matrix products, arithmetic and copies ran while one was open for 13% -> 14% of each run, Pallas kernels for 0% -> 0%
where the time goes in v1:
time: 1330 us; the launch traced here: 1320 us
  waiting for transfers between devices  723 us (54%)
  local copies, waits for them, and re-layouts  238 us (18%)
  other arithmetic  161 us (12%)
  matrix products  156 us (12%)
  starting transfers between devices  23.3 us (2%)
  between operations  14 us (1%)
    psum x2, waiting for transfers between devices, per_device(): updated = step_scale * lax.psum(summed, 'op') - earlier  405 us
    ppermute x14, waiting for transfers between devices, pairwise_exchange(): part = lax.ppermute(part, axis, [(d, d ^ mask) for d in range(ways)])  226 us
    dot_general x2, matrix products, per_device(): jnp.einsum('rjoc,rjcnm->nmro', term_factors, grouped, precision=lax.Preci...  95.9 us
    all_to_all x1, waiting for transfers between devices, per_device(): lax.all_to_all(previous.reshape(row_count, block_count, block_size), 'str...  92.6 us
    select_n x3, other arithmetic, per_device(): jnp.take(received.reshape(block_count, block_size, group_count, item_coun...  69.9 us
    select_n x2, other arithmetic, per_device(): jnp.take(current.reshape(row_count, block_count, block_size), column_list...  68.1 us
    dot_general x2, matrix products, per_device(): jnp.einsum('arjc,rjoc->aro', gathered, term_factors, precision=lax.Precis...  60.4 us
    unnamed x14, local copies, waits for them, and re-layouts  55 us
  transfers between devices with their start and end apart: 17, of which 8 were waited for; matrix products, arithmetic and copies ran while one was open for 14% of the time, Pallas kernels for 0%

profile of v1, /device:TPU:0, one launch (start us, length us, event | category | flops | bytes accessed | tf_op | source)
XLA Modules:
  0.0 1315.8 jit_solution(4811980344420027612)
XLA Ops:
  7.4 9.0 copy.22
  16.4 9.0 copy.23
  25.4 22.3 %gather_fusion = f32[192,512,128]{2,1,0:T(8,128)} fusion(f32[512,32,128]{2,0,1:T(8,128)} %copy.23, s32[1024]{0:T(1024)S(1)} %pad_clamp_fusion), kind=kCustom, calls=%fused_computation.clone | custom fusion | bytes 100664064 | tf_op jit(solution)/shard_map/jit(_take)/gather | solution.py:46
  47.6 34.1 %broadcast_select_fusion.3 = f32[192,512,128]{2,1,0:T(8,128)} fusion(f32[192,512,128]{2,1,0:T(8,128)} %gather_fusion, pred[192]{0:T(512)(128)(4,1)S(1)} %compare_and_fusion), kind=kLoop, calls=%fused_computation.7 | loop fusion | flops 12582912 | bytes 100663488 | tf_op jit(solution)/shard_map/jit(_take)/select_n | solution.py:46
  81.7 30.2 %fusion.8 = f32[32,512,128]{2,1,0:T(8,128)} fusion(f32[512,32,6,128]{3,0,2,1:T(8,128)} %bitcast.112, bf16[1,32,6,128,128]{4,3,2,1,0:T(8,128)(2,1)} %param.10), kind=kOutput, calls=%fused_computation.19 | convolution fusion | flops 19327352832 | bytes 65011712 | tf_op jit(solution)/shard_map/arjc,rjoc->aro/dot_general | solution.py:50
  126.5 61.9 %collective-permute-done.1 = f32[512,4,128]{2,0,1:T(8,128)S(1)} collective-permute-done((f32[512,4,128]{2,0,1:T(8,128)S(1)}, f32[512,4,128]{2,0,1:T(8,128)S(1)}, u32[]{:S(2)}, u32[]{:S(2)}) %collective-permute-start.1) | collective-permute-done | bytes 1048608 | tf_op jit(solution)/shard_map/ppermute | solution.py:21
  190.1 9.0 copy.26
  217.3 42.0 %collective-permute-done.4 = f32[512,4,128]{2,0,1:T(8,128)} collective-permute-done((f32[512,4,128]{2,0,1:T(8,128)S(1)}, f32[512,4,128]{2,0,1:T(8,128)}, u32[]{:S(2)}, u32[]{:S(2)}) %collective-permute-start.4) | collective-permute-done | bytes 1048608 | tf_op jit(solution)/shard_map/ppermute | solution.py:21
  266.0 22.3 %gather_fusion.1 = f32[192,128,4,128]{3,1,2,0:T(8,128)} fusion(f32[32,128,4,128]{3,1,0,2:T(8,128)} %bitcast.14, s32[1024]{0:T(1024)S(1)} %pad_clamp_fusion), kind=kCustom, calls=%fused_computation.1.clone | custom fusion | bytes 100664064 | tf_op jit(solution)/shard_map/jit(_take)/gather | solution.py:56
  288.3 34.9 %broadcast_select_fusion.1 = f32[192,128,4,128]{3,1,2,0:T(8,128)} fusion(f32[192,128,4,128]{3,1,2,0:T(8,128)} %gather_fusion.1, pred[192]{0:T(512)(128)(4,1)S(1)} %compare_and_fusion), kind=kLoop, calls=%fused_computation.5 | loop fusion | flops 12582912 | bytes 100663488 | tf_op jit(solution)/shard_map/jit(_take)/select_n | solution.py:56
  323.2 48.1 %fusion.14 = f32[4,128,32,128]{3,1,0,2:T(8,128)} fusion(f32[32,6,128,4,128]{4,2,3,1,0:T(8,128)} %bitcast.115, bf16[1,32,6,128,128]{4,3,2,1,0:T(8,128)(2,1)} %param.10), kind=kOutput, calls=%fused_computation.21 | convolution fusion | flops 19327352832 | bytes 65011712 | tf_op jit(solution)/shard_map/rjoc,rjcnm->nmro/dot_general | solution.py:60
  371.3 8.2 copy.25
  379.6 11.7 copy.49
  391.3 92.6 %all-to-all-done = f32[512,32,128]{0,2,1:T(8,128)} async-done(((f32[512,32,128]{0,2,1:T(8,128)}), f32[512,32,128]{0,2,1:T(8,128)}, u32[]{:S(2)}, u32[]{:S(2)}) %all-to-all-start) | async-done | bytes 8388640 | tf_op jit(solution)/shard_map/all_to_all | solution.py:34
  492.2 11.7 copy.44
  503.9 190.4 %all-reduce.3.cloned.1.call-done = f32[512,4096]{1,0:T(8,128)} async-done(((f32[512,4096]{1,0:T(8,128)}), f32[512,4096]{1,0:T(8,128)}) %all-reduce.3.cloned.1.call-update) | async-done | bytes 8388624 | tf_op jit(solution)/shard_map/psum | solution.py:65
  694.3 11.3 bitcast_subtract_fusion
  705.6 9.0 copy.29
  714.6 8.9 copy.30
  723.6 22.3 %gather_fusion.2 = f32[192,512,128]{2,1,0:T(8,128)} fusion(f32[512,32,128]{2,0,1:T(8,128)} %copy.30, s32[1024]{0:T(1024)S(1)} %pad_clamp_fusion), kind=kCustom, calls=%fused_computation.2.clone | custom fusion | bytes 100664064 | tf_op jit(solution)/shard_map/jit(_take)/gather | solution.py:46
  745.8 34.1 %broadcast_select_fusion.2 = f32[192,512,128]{2,1,0:T(8,128)} fusion(f32[192,512,128]{2,1,0:T(8,128)} %gather_fusion.2, pred[192]{0:T(512)(128)(4,1)S(1)} %compare_and_fusion), kind=kLoop, calls=%fused_computation.6 | loop fusion | flops 12582912 | bytes 100663488 | tf_op jit(solution)/shard_map/jit(_take)/select_n | solution.py:46
  779.9 30.2 %fusion.11 = f32[32,512,128]{2,1,0:T(8,128)} fusion(f32[512,32,6,128]{3,0,2,1:T(8,128)} %bitcast.113, bf16[1,32,6,128,128]{4,3,2,1,0:T(8,128)(2,1)} %param.10), kind=kOutput, calls=%fused_computation.20 | convolution fusion | flops 19327352832 | bytes 65011712 | tf_op jit(solution)/shard_map/arjc,rjoc->aro/dot_general | solution.py:50
  821.9 62.5 %collective-permute-done.8 = f32[512,4,128]{2,0,1:T(8,128)S(1)} collective-permute-done((f32[512,4,128]{2,0,1:T(8,128)S(1)}, f32[512,4,128]{2,0,1:T(8,128)S(1)}, u32[]{:S(2)}, u32[]{:S(2)}) %collective-permute-start.8) | collective-permute-done | bytes 1048608 | tf_op jit(solution)/shard_map/ppermute | solution.py:21
  892.8 13.0 collective-permute-done.9
  907.9 46.1 %collective-permute-done.11 = f32[512,4,128]{2,0,1:T(8,128)S(1)} collective-permute-done((f32[512,4,128]{2,0,1:T(8,128)S(1)}, f32[512,4,128]{2,0,1:T(8,128)S(1)}, u32[]{:S(2)}, u32[]{:S(2)}) %collective-permute-start.11) | collective-permute-done | bytes 1048608 | tf_op jit(solution)/shard_map/ppermute | solution.py:21
  957.2 22.4 %gather_fusion.3 = f32[192,128,4,128]{3,1,2,0:T(8,128)} fusion(f32[32,128,4,128]{3,1,0,2:T(8,128)} %bitcast.39, s32[1024]{0:T(1024)S(1)} %pad_clamp_fusion), kind=kCustom, calls=%fused_computation.3.clone | custom fusion | bytes 100664064 | tf_op jit(solution)/shard_map/jit(_take)/gather | solution.py:56
  979.6 34.9 %broadcast_select_fusion = f32[192,128,4,128]{3,1,2,0:T(8,128)} fusion(f32[192,128,4,128]{3,1,2,0:T(8,128)} %gather_fusion.3, pred[192]{0:T(512)(128)(4,1)S(1)} %compare_and_fusion), kind=kLoop, calls=%fused_computation.4 | loop fusion | flops 12582912 | bytes 100663488 | tf_op jit(solution)/shard_map/jit(_take)/select_n | solution.py:56
  1014.6 47.8 %fusion.17 = f32[4,128,32,128]{3,1,0,2:T(8,128)} fusion(f32[32,6,128,4,128]{4,2,3,1,0:T(8,128)} %bitcast.114, bf16[1,32,6,128,128]{4,3,2,1,0:T(8,128)(2,1)} %param.10), kind=kOutput, calls=%fused_computation.22 | convolution fusion | flops 19327352832 | bytes 65011712 | tf_op jit(solution)/shard_map/rjoc,rjcnm->nmro/dot_general | solution.py:60
  1062.4 8.2 copy.32
  1070.7 11.8 copy.48
  1082.4 214.8 %all-reduce.5.cloned.1.call-done = f32[512,4096]{1,0:T(8,128)} async-done(((f32[512,4096]{1,0:T(8,128)}), f32[512,4096]{1,0:T(8,128)}) %all-reduce.5.cloned.1.call-update) | async-done | bytes 8388624 | tf_op jit(solution)/shard_map/psum | solution.py:65
  1297.3 11.3 sub.7
  (62 shorter events, 75.7 us)
Async XLA Ops:
  117.0 5.9 collective-permute-start
  117.5 70.9 %collective-permute-start.1 = (f32[512,4,128]{2,0,1:T(8,128)S(1)}, f32[512,4,128]{2,0,1:T(8,128)S(1)}, u32[]{:S(2)}, u32[]{:S(2)}) collective-permute-start(f32[512,4,128]{2,0,1:T(8,128)S(1)} %get-tuple-element.19), channel_id=1, source_target_pairs={{0,2},{1,3},{2,0},{3,1},{4,6},{5,7},{6,4},{7,5},{8,10},{9,11},{10,... | collective-permute-start | bytes 3145736 | tf_op jit(solution)/shard_map/ppermute | solution.py:21
  120.0 92.7 %collective-permute-start.2 = (f32[512,4,128]{2,0,1:T(8,128)}, f32[512,4,128]{2,0,1:T(8,128)}, u32[]{:S(2)}, u32[]{:S(2)}) collective-permute-start(f32[512,4,128]{2,0,1:T(8,128)} %get-tuple-element.18), channel_id=1, source_target_pairs={{0,3},{1,2},{2,1},{3,0},{4,7},{5,6},{6,5},{7,4},{8,11},{9,10},{10,... | collective-permute-start | bytes 3145736 | tf_op jit(solution)/shard_map/ppermute | solution.py:21
  120.1 94.9 %collective-permute-start.3 = (f32[512,4,128]{2,0,1:T(8,128)}, f32[512,4,128]{2,0,1:T(8,128)}, u32[]{:S(2)}, u32[]{:S(2)}) collective-permute-start(f32[512,4,128]{2,0,1:T(8,128)} %get-tuple-element.17), channel_id=1, source_target_pairs={{0,4},{1,5},{2,6},{3,7},{4,0},{5,1},{6,2},{7,3},{8,12},{9,13},{10,... | collective-permute-start | bytes 3145736 | tf_op jit(solution)/shard_map/ppermute | solution.py:21
  122.9 136.3 %collective-permute-start.4 = (f32[512,4,128]{2,0,1:T(8,128)S(1)}, f32[512,4,128]{2,0,1:T(8,128)}, u32[]{:S(2)}, u32[]{:S(2)}) collective-permute-start(f32[512,4,128]{2,0,1:T(8,128)S(1)} %get-tuple-element.16), channel_id=1, source_target_pairs={{0,5},{1,4},{2,7},{3,6},{4,1},{5,0},{6,3},{7,2},{8,13},{9,12},{10,... | collective-permute-start | bytes 3145736 | tf_op jit(solution)/shard_map/ppermute | solution.py:21
  122.9 65.5 %copy-start = (f32[512,4,128]{2,0,1:T(8,128)}, f32[512,4,128]{2,0,1:T(8,128)S(1)}, u32[]{:S(2)}) copy-start(f32[512,4,128]{2,0,1:T(8,128)S(1)} %collective-permute-done) | copy-start | bytes 3145732
  122.9 138.6 %collective-permute-start.5 = (f32[512,4,128]{2,0,1:T(8,128)S(1)}, f32[512,4,128]{2,0,1:T(8,128)}, u32[]{:S(2)}, u32[]{:S(2)}) collective-permute-start(f32[512,4,128]{2,0,1:T(8,128)S(1)} %get-tuple-element.15), channel_id=1, source_target_pairs={{0,6},{1,7},{2,4},{3,5},{4,2},{5,3},{6,0},{7,1},{8,14},{9,15},{10,... | collective-permute-start | bytes 3145736 | tf_op jit(solution)/shard_map/ppermute | solution.py:21
  188.4 1.1 copy-start.2
  189.4 74.4 %collective-permute-start.6 = (f32[512,4,128]{2,0,1:T(8,128)S(1)}, f32[512,4,128]{2,0,1:T(8,128)}, u32[]{:S(2)}, u32[]{:S(2)}) collective-permute-start(f32[512,4,128]{2,0,1:T(8,128)S(1)} %get-tuple-element.14), channel_id=1, source_target_pairs={{0,7},{1,6},{2,5},{3,4},{4,3},{5,2},{6,1},{7,0},{8,15},{9,14},{10,... | collective-permute-start | bytes 3145736 | tf_op jit(solution)/shard_map/ppermute | solution.py:21
  199.1 284.9 %all-to-all-start = ((f32[512,32,128]{0,2,1:T(8,128)}), f32[512,32,128]{0,2,1:T(8,128)}, u32[]{:S(2)}, u32[]{:S(2)}) async-start(f32[512,32,128]{0,2,1:T(8,128)} %bitcast.117), calls=%async_computation | async-start | bytes 16777216 | tf_op jit(solution)/shard_map/all_to_all | solution.py:34
  204.1 490.2 %all-reduce.3.cloned.1.call-start = ((), (), s32[]{:S(2)}) async-start(), calls=%async_computation.1 | async-start | bytes 16777216 | tf_op jit(solution)/shard_map/psum | solution.py:65
  204.4 6.2 copy-start.1
  204.4 7.3 copy-start.3
  391.3 906.0 %all-reduce.5.cloned.1.call-start = ((), (), s32[]{:S(2)}) async-start(), calls=%async_computation.2 | async-start | bytes 16777216 | tf_op jit(solution)/shard_map/psum | solution.py:65
  814.0 4.5 collective-permute-start.7
  814.1 70.3 %collective-permute-start.8 = (f32[512,4,128]{2,0,1:T(8,128)S(1)}, f32[512,4,128]{2,0,1:T(8,128)S(1)}, u32[]{:S(2)}, u32[]{:S(2)}) collective-permute-start(f32[512,4,128]{2,0,1:T(8,128)S(1)} %get-tuple-element.12), channel_id=1, source_target_pairs={{0,2},{1,3},{2,0},{3,1},{4,6},{5,7},{6,4},{7,5},{8,10},{9,11},{10,... | collective-permute-start | bytes 3145736 | tf_op jit(solution)/shard_map/ppermute | solution.py:21
  815.6 90.2 %collective-permute-start.9 = (f32[512,4,128]{2,0,1:T(8,128)S(1)}, f32[512,4,128]{2,0,1:T(8,128)S(1)}, u32[]{:S(2)}, u32[]{:S(2)}) collective-permute-start(f32[512,4,128]{2,0,1:T(8,128)S(1)} %get-tuple-element.11), channel_id=1, source_target_pairs={{0,3},{1,2},{2,1},{3,0},{4,7},{5,6},{6,5},{7,4},{8,11},{9,10},{10,... | collective-permute-start | bytes 3145736 | tf_op jit(solution)/shard_map/ppermute | solution.py:21
  815.9 90.9 %collective-permute-start.10 = (f32[512,4,128]{2,0,1:T(8,128)S(1)}, f32[512,4,128]{2,0,1:T(8,128)S(1)}, u32[]{:S(2)}, u32[]{:S(2)}) collective-permute-start(f32[512,4,128]{2,0,1:T(8,128)S(1)} %get-tuple-element.10), channel_id=1, source_target_pairs={{0,4},{1,5},{2,6},{3,7},{4,0},{5,1},{6,2},{7,3},{8,12},{9,13},{10,... | collective-permute-start | bytes 3145736 | tf_op jit(solution)/shard_map/ppermute | solution.py:21
  818.3 135.7 %collective-permute-start.11 = (f32[512,4,128]{2,0,1:T(8,128)S(1)}, f32[512,4,128]{2,0,1:T(8,128)S(1)}, u32[]{:S(2)}, u32[]{:S(2)}) collective-permute-start(f32[512,4,128]{2,0,1:T(8,128)S(1)} %get-tuple-element.9), channel_id=1, source_target_pairs={{0,5},{1,4},{2,7},{3,6},{4,1},{5,0},{6,3},{7,2},{8,13},{9,12},{10,... | collective-permute-start | bytes 3145736 | tf_op jit(solution)/shard_map/ppermute | solution.py:21
  818.6 136.5 %collective-permute-start.12 = (f32[512,4,128]{2,0,1:T(8,128)S(1)}, f32[512,4,128]{2,0,1:T(8,128)S(1)}, u32[]{:S(2)}, u32[]{:S(2)}) collective-permute-start(f32[512,4,128]{2,0,1:T(8,128)S(1)} %get-tuple-element.8), channel_id=1, source_target_pairs={{0,6},{1,7},{2,4},{3,5},{4,2},{5,3},{6,0},{7,1},{8,14},{9,15},{10,... | collective-permute-start | bytes 3145736 | tf_op jit(solution)/shard_map/ppermute | solution.py:21
  884.4 71.7 %collective-permute-start.13 = (f32[512,4,128]{2,0,1:T(8,128)S(1)}, f32[512,4,128]{2,0,1:T(8,128)S(1)}, u32[]{:S(2)}, u32[]{:S(2)}) collective-permute-start(f32[512,4,128]{2,0,1:T(8,128)S(1)} %get-tuple-element.6), channel_id=1, source_target_pairs={{0,7},{1,6},{2,5},{3,4},{4,3},{5,2},{6,1},{7,0},{8,15},{9,14},{10,... | collective-permute-start | bytes 3145736 | tf_op jit(solution)/shard_map/ppermute | solution.py:21
Sparse Core Ops, SparseCore 0:
  391.4 302.8 all-reduce.2
  1082.6 214.6 all-reduce.4
